TPU v7x, 32 devices: a whole 2x2x4 slice. The times are simulated.
32 devices in a mesh: dp: 16 (over z, x, core), tensor: 2 (over y).
Axes of the slice: x: 2, y: 2, z: 4, core: 2. Of those that a mesh axis runs over, the one named last changes fastest.
Arguments:
- inputs: bfloat16 [16384, 768], P(('dp', 'tensor')), may hold values from -6 to 6
- grad_out: bfloat16 [16384, 768], P(('dp', 'tensor')), may hold values from -6 to 6
- page_lengths: int32 [16, 6], P('dp'), may hold values from 0 to 1024, as said below
- gain_one: bfloat16 [768], replicated, may hold values from 0.5 to 1.5
- gain_two: bfloat16 [768], replicated, may hold values from 0.5 to 1.5
- w_query: bfloat16 [768, 768], P(None, 'tensor'), may hold values from -0.21875 to 0.21875
- w_key: bfloat16 [768, 768], P(None, 'tensor'), may hold values from -0.21875 to 0.21875
- w_value: bfloat16 [768, 768], P(None, 'tensor'), may hold values from -0.21875 to 0.21875
- w_out: bfloat16 [768, 768], P('tensor'), may hold values from -3.5 to 3.5
- w_up: bfloat16 [768, 3072], P(None, 'tensor'), may hold values from -0.21875 to 0.21875
- w_down: bfloat16 [3072, 768], P('tensor'), may hold values from -0.109375 to 0.109375
- rel_table: bfloat16 [12, 16], P('tensor'), may hold values from -4 to 4
Outputs:
- out: bfloat16 [16384, 768], P(('dp', 'tensor'))
- input_grad: bfloat16 [16384, 768], P(('dp', 'tensor'))
- gain_one_grad: float32 [768], replicated
- gain_two_grad: float32 [768], replicated
- query_grad: float32 [768, 768], P(None, 'tensor')
- key_grad: float32 [768, 768], P(None, 'tensor')
- value_grad: float32 [768, 768], P(None, 'tensor')
- out_proj_grad: float32 [768, 768], P('tensor')
- up_grad: float32 [768, 3072], P(None, 'tensor')
- down_grad: float32 [3072, 768], P('tensor')
- table_grad: float32 [12, 16], P('tensor')
Inputs may be any that keep to these rules, and one draw needn't show every extreme that they name: `page_lengths`: each row of a group lists pages of one resolution, all of 196, all of 576 or all of 1024 patches, as many as fit in 1024, then one slot with the remaining patches (possibly 0), then zeros; each row sums to 1024, and some group holds pages of 1024.
All inputs are finite; a program needn't handle non-finite values.
Results may differ from a plain program's by a relative error of at most 0.017.
Values may be sent and summed in bfloat16 or wider, within the bound.
No kernel may reach another device: no remote copies, remote signals or barrier semaphores. Data moves between devices by JAX's collectives and lax.ppermute only.
A program may use at most 192 MiB of HBM per device.

v0:
```python
import jax
import jax.numpy as jnp
from jax import lax
from jax.sharding import PartitionSpec as P

HEAD_DIM = 64
BLOCK = 512
BUCKETS = 16


def layer_norm(values, gain):
    centred = values - jnp.mean(values, axis=-1, keepdims=True)
    variance = jnp.mean(centred * centred, axis=-1, keepdims=True)
    return centred * lax.rsqrt(variance + 1e-05) * gain


def gelu_tanh(values):
    return jax.nn.gelu(values, approximate=True)


def plain_times(left_side, right_side):
    return jnp.dot(left_side, right_side, preferred_element_type=jnp.float32)


def times_transposed(left_side, right_side):
    return lax.dot_general(
        left_side, right_side, (((1,), (1,)), ((), ())), preferred_element_type=jnp.float32
    )


def transposed_times(left_side, right_side):
    return lax.dot_general(
        left_side, right_side, (((0,), (0,)), ((), ())), preferred_element_type=jnp.float32
    )


def relative(first_row, key_count):
    half_count = BUCKETS // 2
    row_pos = first_row + jnp.arange(BLOCK, dtype=jnp.int32)
    offsets = row_pos[:, None] - jnp.arange(key_count, dtype=jnp.int32)[None, :]
    distance = jnp.abs(offsets) + 1
    levels = jnp.zeros_like(offsets)
    for exponent in range(1, half_count):
        levels = levels + (distance >= 2**exponent).astype(jnp.int32)
    buckets = levels + half_count * (offsets < 0).astype(jnp.int32)
    return (buckets[:, :, None] == jnp.arange(BUCKETS, dtype=jnp.int32)[None, None, :]).astype(
        jnp.bfloat16
    )


def body(
    inputs,
    grad_out,
    page_lengths,
    gain_one,
    gain_two,
    w_query,
    w_key,
    w_value,
    w_out,
    w_up,
    w_down,
    rel_table,
):
    local_heads = w_query.shape[1] // HEAD_DIM
    score_scale = HEAD_DIM ** (-0.5)
    gain_first = gain_one.astype(jnp.float32)
    gain_second = gain_two.astype(jnp.float32)
    tokens = inputs.astype(jnp.float32)
    normed_own = layer_norm(tokens, gain_first).astype(jnp.bfloat16)
    normed = lax.all_gather(normed_own, "tensor", axis=0, tiled=True)
    group_rows = normed.shape[0]
    heads_view = (group_rows, local_heads, HEAD_DIM)
    query_heads = plain_times(normed, w_query).astype(jnp.bfloat16).reshape(heads_view)
    key_heads = plain_times(normed, w_key).astype(jnp.bfloat16).reshape(heads_view)
    value_heads = plain_times(normed, w_value).astype(jnp.bfloat16).reshape(heads_view)
    page_ends = jnp.cumsum(page_lengths[0])
    positions = jnp.arange(group_rows, dtype=jnp.int32)
    page_of = jnp.sum((positions[:, None] >= page_ends[None, :]).astype(jnp.int32), axis=1)

    def block_scores(first_row):
        query_block = lax.dynamic_slice_in_dim(query_heads, first_row, BLOCK, 0)
        raw_scores = (
            jnp.einsum("qhd,khd->hqk", query_block, key_heads, preferred_element_type=jnp.float32)
            * score_scale
        )
        one_hot = relative(first_row, group_rows)
        bias = jnp.einsum("qkm,hm->hqk", one_hot, rel_table, preferred_element_type=jnp.float32)
        scores = raw_scores + bias
        same_page = (
            lax.dynamic_slice_in_dim(page_of, first_row, BLOCK, 0)[:, None] == page_of[None, :]
        )
        scores = jnp.where(same_page[None], scores, -1e30)
        return (query_block, scores, one_hot)

    def attend(first_row):
        scores = block_scores(first_row)[1]
        log_total = jax.nn.logsumexp(scores, axis=-1)
        weight = jnp.exp(scores - log_total[..., None]).astype(jnp.bfloat16)
        block_out = jnp.einsum(
            "hqk,khd->qhd", weight, value_heads, preferred_element_type=jnp.float32
        )
        return (block_out.astype(jnp.bfloat16), log_total)

    starts = jnp.arange(group_rows // BLOCK, dtype=jnp.int32) * BLOCK
    attended_blocks, log_totals = lax.map(attend, starts)
    attended = attended_blocks.reshape(group_rows, local_heads * HEAD_DIM)
    branch_one = lax.psum_scatter(
        plain_times(attended, w_out), "tensor", scatter_dimension=0, tiled=True
    )
    middle = tokens + branch_one
    normed_two_own = layer_norm(middle, gain_second).astype(jnp.bfloat16)
    normed_two = lax.all_gather(normed_two_own, "tensor", axis=0, tiled=True)
    up_use, down_use = (w_up, w_down)
    pre_act = plain_times(normed_two, up_use)
    hidden = gelu_tanh(pre_act).astype(jnp.bfloat16)
    branch_two = lax.psum_scatter(
        plain_times(hidden, down_use).astype(jnp.bfloat16),
        "tensor",
        scatter_dimension=0,
        tiled=True,
    ).astype(jnp.float32)
    grad_rows = lax.all_gather(grad_out, "tensor", axis=0, tiled=True)
    out = (middle + branch_two).astype(jnp.bfloat16)
    down_part = transposed_times(hidden, grad_rows)
    grad_hidden = times_transposed(grad_rows, down_use)
    gelu_back = jax.vjp(gelu_tanh, pre_act)[1]
    grad_pre = gelu_back(grad_hidden)[0].astype(jnp.bfloat16)
    up_part = transposed_times(normed_two, grad_pre)
    grad_normed_two = lax.psum_scatter(
        times_transposed(grad_pre, w_up).astype(jnp.bfloat16),
        "tensor",
        scatter_dimension=0,
        tiled=True,
    ).astype(jnp.float32)
    up_final, down_final = (up_part, down_part)
    norm_two_back = jax.vjp(layer_norm, middle, gain_second)[1]
    grad_middle_norm, gain_two_part = norm_two_back(grad_normed_two)
    grad_middle = grad_out.astype(jnp.float32) + grad_middle_norm
    grad_branch = lax.all_gather(grad_middle.astype(jnp.bfloat16), "tensor", axis=0, tiled=True)
    out_proj_grad = transposed_times(attended, grad_branch)
    grad_attended = times_transposed(grad_branch, w_out).astype(jnp.bfloat16).reshape(heads_view)

    def attend_back(carry, block_pair):
        key_acc, value_acc, table_acc = carry
        first_row, log_total = block_pair
        query_block, scores, one_hot = block_scores(first_row)
        prob = jnp.exp(scores - log_total[..., None])
        prob_low = prob.astype(jnp.bfloat16)
        grad_block = lax.dynamic_slice_in_dim(grad_attended, first_row, BLOCK, 0)
        grad_prob = jnp.einsum(
            "qhd,khd->hqk", grad_block, value_heads, preferred_element_type=jnp.float32
        )
        row_inner = jnp.sum(prob * grad_prob, axis=-1, keepdims=True)
        grad_scores = prob * (grad_prob - row_inner)
        table_step = jnp.einsum(
            "hqk,qkm->hm", grad_scores, one_hot.astype(jnp.float32), precision=lax.Precision.HIGH
        )
        scores_low = grad_scores.astype(jnp.bfloat16)
        grad_query = (
            jnp.einsum("hqk,khd->qhd", scores_low, key_heads, preferred_element_type=jnp.float32)
            * score_scale
        )
        key_acc = (
            key_acc
            + jnp.einsum(
                "hqk,qhd->khd", scores_low, query_block, preferred_element_type=jnp.float32
            )
            * score_scale
        )
        value_acc = value_acc + jnp.einsum(
            "hqk,qhd->khd", prob_low, grad_block, preferred_element_type=jnp.float32
        )
        table_acc = table_acc + table_step
        return ((key_acc, value_acc, table_acc), grad_query.astype(jnp.bfloat16))

    zero_heads = jnp.zeros(heads_view, jnp.float32)
    zero_table = jnp.zeros((local_heads, BUCKETS), jnp.float32)
    (key_sum, value_sum, table_part), query_blocks = lax.scan(
        attend_back, (zero_heads, zero_heads, zero_table), (starts, log_totals)
    )
    flat_width = local_heads * HEAD_DIM
    grad_query = query_blocks.reshape(group_rows, flat_width)
    grad_key = key_sum.astype(jnp.bfloat16).reshape(group_rows, flat_width)
    grad_value = value_sum.astype(jnp.bfloat16).reshape(group_rows, flat_width)
    query_part = transposed_times(normed, grad_query)
    key_part = transposed_times(normed, grad_key)
    value_part = transposed_times(normed, grad_value)
    total = times_transposed(grad_query, w_query)
    total = total + times_transposed(grad_key, w_key)
    grad_normed_one = lax.psum_scatter(
        (total + times_transposed(grad_value, w_value)).astype(jnp.bfloat16),
        "tensor",
        scatter_dimension=0,
        tiled=True,
    ).astype(jnp.float32)
    norm_one_back = jax.vjp(layer_norm, tokens, gain_first)[1]
    grad_tokens, gain_one_part = norm_one_back(grad_normed_one)
    input_grad = (grad_middle + grad_tokens).astype(jnp.bfloat16)
    summed = lax.psum(
        (query_part, key_part, value_part, out_proj_grad, up_final, down_final, table_part), "dp"
    )
    query_total, key_total, value_total, out_total, up_total, down_total, table_total = summed
    gain_sums = lax.psum((gain_one_part, gain_two_part), ("dp", "tensor"))
    return (
        out,
        input_grad,
        gain_sums[0],
        gain_sums[1],
        query_total,
        key_total,
        value_total,
        out_total,
        up_total,
        down_total,
        table_total,
    )


def solution(mesh):
    in_specs = (
        P(("dp", "tensor"), None),
        P(("dp", "tensor"), None),
        P("dp", None),
        P(),
        P(),
        P(None, "tensor"),
        P(None, "tensor"),
        P(None, "tensor"),
        P("tensor", None),
        P(None, "tensor"),
        P("tensor", None),
        P("tensor", None),
    )
    out_specs = (
        P(("dp", "tensor"), None),
        P(("dp", "tensor"), None),
        P(),
        P(),
        P(None, "tensor"),
        P(None, "tensor"),
        P(None, "tensor"),
        P("tensor", None),
        P(None, "tensor"),
        P("tensor", None),
        P("tensor", None),
    )
    return jax.shard_map(body, mesh=mesh, in_specs=in_specs, out_specs=out_specs, check_vma=False)
```

profile of v0, /device:TPU:0, one launch (start us, length us, event | category | flops | bytes accessed | tf_op | source)
XLA Modules:
  0.0 885.2 jit_solution(784256954340176046)
XLA Ops:
  13.7 29.7 %all-gather.5.cloned.1.call-done = bf16[1024,768]{1,0:T(8,128)(2,1)} async-done(((bf16[512,768]{1,0:T(8,128)(2,1)}), bf16[1024,768]{1,0:T(8,128)(2,1)}) %all-gather.5.cloned.1.call-update) | async-done | bytes 1572880 | tf_op jit(solution)/shard_map/all_gather | solution.py:71
  51.4 84.2 %while.29 = (s32[]{:T(128)}, bf16[2,512,6,64]{1,3,2,0:T(8,128)(2,1)}, f32[2,6,512]{2,1,0:T(8,128)S(1)}, s32[2]{0:T(128)S(1)}, s32[1024]{0:T(1024)S(1)}, /*index=...) while((s32[]{:T(128)}, ...), condition=%wide.region_7.8_spmd, body=%wide.region_4.7_spmd.sunk | while | flops 953901568 | bytes 133609992 | solution.py:106
  57.3 8.4 fusion.175
  65.7 15.3 %fusion.176 = (f32[6,512]{1,0:T(8,128)S(1)}, f32[6,512,1024]{2,1,0:T(8,128)S(1)}) fusion(f32[512,1024,6]{1,2,0:T(8,128)} %fusion.175, bf16[1024,6,64]{0,2,1:T(8,128)(2,1)S(1)} %get-tuple-element.416, bf16[1024,6,64]{0,2,1:T(8,128)(2,1)S(1)} %copy-done.8, s32[]{:T(128)S(6)} %select_n.59, pred[512,1024]{1,0:T(8,128)(4,1)S(1)} %broadcast_compare_fusion.4), kind=kOutput, calls=%fused_computation.146.clone.1 | convolution fusion | flops 415233024 | bytes 26882052 | tf_op jit(solution)/shard_map/while/body/eval_jaxpr/qhd,khd->hqk/dot_general | solution.py:84
  99.1 8.4 fusion.175
  107.5 15.3 %fusion.176 = (f32[6,512]{1,0:T(8,128)S(1)}, f32[6,512,1024]{2,1,0:T(8,128)S(1)}) fusion(f32[512,1024,6]{1,2,0:T(8,128)} %fusion.175, bf16[1024,6,64]{0,2,1:T(8,128)(2,1)S(1)} %get-tuple-element.416, bf16[1024,6,64]{0,2,1:T(8,128)(2,1)S(1)} %copy-done.8, s32[]{:T(128)S(6)} %select_n.59, pred[512,1024]{1,0:T(8,128)(4,1)S(1)} %broadcast_compare_fusion.4), kind=kOutput, calls=%fused_computation.146.clone.1 | convolution fusion | flops 415233024 | bytes 26882052 | tf_op jit(solution)/shard_map/while/body/eval_jaxpr/qhd,khd->hqk/dot_general | solution.py:84
  142.2 42.7 %reduce-scatter.5.cloned.1.call-done = f32[512,768]{1,0:T(8,128)} async-done(((f32[1024,768]{1,0:T(8,128)}), f32[512,768]{1,0:T(8,128)}) %reduce-scatter.5.cloned.1.call-update) | async-done | bytes 1572880 | tf_op jit(solution)/shard_map/reduce_scatter | solution.py:108
  189.1 24.7 %all-gather.9.cloned.1.call-done = bf16[1024,768]{1,0:T(8,128)(2,1)} async-done(((bf16[512,768]{1,0:T(8,128)(2,1)}), bf16[1024,768]{1,0:T(8,128)(2,1)}) %all-gather.9.cloned.1.call-update) | async-done | bytes 1572880 | tf_op jit(solution)/shard_map/all_gather | solution.py:123
  213.8 7.5 fusion.101
  221.2 21.8 %all-gather.7.cloned.1.call-done = bf16[1024,768]{1,0:T(8,128)(2,1)} async-done(((bf16[512,768]{1,0:T(8,128)(2,1)}), bf16[1024,768]{1,0:T(8,128)(2,1)}) %all-gather.7.cloned.1.call-update) | async-done | bytes 1572880 | tf_op jit(solution)/shard_map/all_gather | solution.py:113
  243.1 9.7 %fusion.77 = (bf16[1024,1536]{1,0:T(8,128)(2,1)S(1)}, f32[1024,1536]{1,0:T(8,128)}) fusion(f32[1024,1536]{1,0:T(8,128)} %fusion.101, bf16[1024,768]{1,0:T(8,128)(2,1)} %all-gather.7.cloned.1.call-done, bf16[768,1536]{1,0:T(8,128)(2,1)S(1)} %copy-done), kind=kOutput, calls=%fused_computation.91 | convolution fusion | flops 2447376384 | bytes 19660800 | tf_op jit(solution)/shard_map/dot_general | solution.py:22
  258.2 8.4 convolution_convert_fusion.1
  266.7 17.7 %reduce-scatter.9.cloned.1.call-done = bf16[512,768]{1,0:T(8,128)(2,1)} async-done(((bf16[1024,768]{1,0:T(8,128)(2,1)}), bf16[512,768]{1,0:T(8,128)(2,1)}) %reduce-scatter.9.cloned.1.call-update) | async-done | bytes 786448 | tf_op jit(solution)/shard_map/reduce_scatter | solution.py:130
  286.9 25.8 %reduce-scatter.7.cloned.1.call-done = bf16[512,768]{1,0:T(8,128)(2,1)} async-done(((bf16[1024,768]{1,0:T(8,128)(2,1)}), bf16[512,768]{1,0:T(8,128)(2,1)}) %reduce-scatter.7.cloned.1.call-update) | async-done | bytes 786448 | tf_op jit(solution)/shard_map/reduce_scatter | solution.py:117
  318.0 27.3 %all-gather.11.cloned.1.call-done = bf16[1024,768]{1,0:T(8,128)(2,1)} async-done(((bf16[512,768]{1,0:T(8,128)(2,1)}), bf16[1024,768]{1,0:T(8,128)(2,1)}) %all-gather.11.cloned.1.call-update) | async-done | bytes 1572880 | tf_op jit(solution)/shard_map/all_gather | solution.py:140
  349.3 214.7 %while.30 = (s32[]{:T(128)}, f32[1024,6,64]{0,2,1:T(8,128)}, f32[1024,6,64]{0,2,1:T(8,128)}, f32[6,16]{1,0:T(8,128)S(1)}, bf16[2,512,6,64]{1,3,2,0:T(8,128)(2,1)...) while((s32[]{:T(128)}, f32[1024,6,64]{0,2,1:T(8,128)}, ...), condition=%wide.region_17.18_spmd.clone, body=%wide.region_15.17_spmd.clone.sunk | while | flops 2483812096 | bytes 329461056 | solution.py:179
  362.7 8.5 fusion.192
  371.2 15.7 %copy.43 = f32[512,1024,6]{1,0,2:T(8,128)} copy(f32[512,1024,6]{0,2,1:T(8,128)} %fusion.192) | data formatting | bytes 25165824 | tf_op jit(solution)/shard_map/while/body/eval_jaxpr/qkm,hm->hqk/dot_general | solution.py:88
  386.9 13.8 %multiply_reduce_fusion.3 = (f32[6,512]{1,0:T(8,128)S(1)}, f32[6,512,1024]{2,1,0:T(8,128)}) fusion(f32[6,512,1024]{2,1,0:T(8,128)} %fusion.191, f32[6,512]{1,0:T(8,128)S(1)} %dynamic-slice_bitcast_fusion.2, f32[512,1024,6]{1,0,2:T(8,128)} %copy.43, bf16[1024,6,64]{0,2,1:T(8,128)(2,1)S(1)} %get-tuple-element.462, ...), kind=kOutput, calls=%fused_computation.44.clone.1 | convolution fusion | flops 421524480 | bytes 39477252 | tf_op jit(solution)/shard_map/while/body/eval_jaxpr/qhd,khd->hqk/dot_general | solution.py:84
  400.7 9.1 %subtract_multiply_fusion.2 = f32[6,512,1024]{2,1,0:T(8,128)S(1)} fusion(f32[6,512,1024]{2,1,0:T(8,128)} %get-tuple-element.384, f32[6,512,1024]{2,1,0:T(8,128)} %fusion.191, f32[6,512]{1,0:T(8,128)S(1)} %get-tuple-element.385), kind=kLoop, calls=%fused_computation.43.clone.1 | loop fusion | flops 6291456 | bytes 37761024 | tf_op jit(solution)/shard_map/while/body/eval_jaxpr/mul | solution.py:155
  422.0 16.0 %copy.44 = f32[6,512,1024]{1,0,2:T(8,128)} copy(f32[6,512,1024]{2,1,0:T(8,128)} %copy-done.2) | data formatting | bytes 25165824 | tf_op jit(solution)/shard_map/while/body/eval_jaxpr/mul | solution.py:155
  437.9 17.4 %fusion.193 = f32[6,16]{1,0:T(8,128)S(1)} fusion(f32[6,512,1024]{1,0,2:T(8,128)} %copy.44, s32[512,1024]{0,1:T(8,128)S(1)} %select_add_fusion.5, f32[6,16]{1,0:T(8,128)S(1)} %get-tuple-element.441, pred[]{:T(512)S(6)} %compare.3), kind=kOutput, calls=%fused_computation.69.clone.1 | convolution fusion | flops 310378688 | bytes 14680833 | tf_op jit(solution)/shard_map/while/body/eval_jaxpr/hqk,qkm->hm/dot_general | solution.py:156
  468.6 8.5 fusion.192
  477.1 15.7 %copy.43 = f32[512,1024,6]{1,0,2:T(8,128)} copy(f32[512,1024,6]{0,2,1:T(8,128)} %fusion.192) | data formatting | bytes 25165824 | tf_op jit(solution)/shard_map/while/body/eval_jaxpr/qkm,hm->hqk/dot_general | solution.py:88
  492.8 13.8 %multiply_reduce_fusion.3 = (f32[6,512]{1,0:T(8,128)S(1)}, f32[6,512,1024]{2,1,0:T(8,128)}) fusion(f32[6,512,1024]{2,1,0:T(8,128)} %fusion.191, f32[6,512]{1,0:T(8,128)S(1)} %dynamic-slice_bitcast_fusion.2, f32[512,1024,6]{1,0,2:T(8,128)} %copy.43, bf16[1024,6,64]{0,2,1:T(8,128)(2,1)S(1)} %get-tuple-element.462, ...), kind=kOutput, calls=%fused_computation.44.clone.1 | convolution fusion | flops 421524480 | bytes 39477252 | tf_op jit(solution)/shard_map/while/body/eval_jaxpr/qhd,khd->hqk/dot_general | solution.py:84
  506.6 9.1 %subtract_multiply_fusion.2 = f32[6,512,1024]{2,1,0:T(8,128)S(1)} fusion(f32[6,512,1024]{2,1,0:T(8,128)} %get-tuple-element.384, f32[6,512,1024]{2,1,0:T(8,128)} %fusion.191, f32[6,512]{1,0:T(8,128)S(1)} %get-tuple-element.385), kind=kLoop, calls=%fused_computation.43.clone.1 | loop fusion | flops 6291456 | bytes 37761024 | tf_op jit(solution)/shard_map/while/body/eval_jaxpr/mul | solution.py:155
  530.4 16.0 %copy.44 = f32[6,512,1024]{1,0,2:T(8,128)} copy(f32[6,512,1024]{2,1,0:T(8,128)} %copy-done.2) | data formatting | bytes 25165824 | tf_op jit(solution)/shard_map/while/body/eval_jaxpr/mul | solution.py:155
  546.4 17.4 %fusion.193 = f32[6,16]{1,0:T(8,128)S(1)} fusion(f32[6,512,1024]{1,0,2:T(8,128)} %copy.44, s32[512,1024]{0,1:T(8,128)S(1)} %select_add_fusion.5, f32[6,16]{1,0:T(8,128)S(1)} %get-tuple-element.441, pred[]{:T(512)S(6)} %compare.3), kind=kOutput, calls=%fused_computation.69.clone.1 | convolution fusion | flops 310378688 | bytes 14680833 | tf_op jit(solution)/shard_map/while/body/eval_jaxpr/hqk,qkm->hm/dot_general | solution.py:156
  579.7 8.8 fusion.96
  596.5 35.2 %psum.71 = f32[6,16]{1,0:T(8,128)} all-reduce(f32[6,16]{1,0:T(8,128)S(1)} %get-tuple-element.134), channel_id=1, replica_groups=mesh['dp'=16,'tensor'=2] {'dp'}, use_global_device_ids=true, to_apply=%region_31.32 | all-reduce | flops 96 | bytes 768 | tf_op jit(solution)/shard_map/psum | solution.py:200
  635.4 38.2 %all-reduce = (f32[768]{0:T(1024)}, f32[768]{0:T(1024)}) all-reduce(f32[768]{0:T(1024)S(1)} %get-tuple-element.179, f32[768]{0:T(1024)S(1)} %copy-done.45), channel_id=1, replica_groups=mesh['dp'=16,'tensor'=2] {'dp','tensor'}, use_global_device_ids=true, to_apply=%region_22.23 | all-reduce | flops 1536 | bytes 12288 | tf_op jit(solution)/shard_map/psum | solution.py:204
  676.4 189.9 %all-reduce.4.cloned.1.call-done = (f32[768,384]{1,0:T(8,128)}, f32[768,384]{1,0:T(8,128)}, f32[768,384]{1,0:T(8,128)}, f32[384,768]{1,0:T(8,128)}, f32[768,1536]{1,0:T(8,128)}, /*index=5*/f32[1536,768]{1,0:T(8,128)}) async-done(((f32[768,384]{1,0:T(8,128)}, f32[768,384]{1,0:T(8,128)}, f32[768,384]{1,0:T(8,128)}, f32[384,768]{1,0:T(8,128)}, f32[768,1536]{1,0:T(8,128)}, /*index=5*/f32[1536,768]{1,0:T(8,128)}), ...) | async-done | bytes 14155792 | tf_op jit(solution)/shard_map/psum | solution.py:200
  (245 shorter events, 165.4 us)
Async XLA Ops:
  7.2 235.9 %copy-start = (bf16[768,1536]{1,0:T(8,128)(2,1)S(1)}, bf16[768,1536]{1,0:T(8,128)(2,1)}, u32[]{:S(2)}) copy-start(bf16[768,1536]{1,0:T(8,128)(2,1)} %param.25) | copy-start | bytes 7077892
  7.2 36.2 %all-gather.5.cloned.1.call-start = ((), (), s32[]{:S(2)}) async-start(), calls=%async_computation.4 | async-start | bytes 2359296 | tf_op jit(solution)/shard_map/all_gather | solution.py:71
  13.3 171.6 %reduce-scatter.5.cloned.1.call-start = ((), (), s32[]{:S(2)}) async-start(), calls=%async_computation.5 | async-start | bytes 4718592 | tf_op jit(solution)/shard_map/reduce_scatter | solution.py:108
  57.3 8.4 copy-start.8
  99.1 8.4 copy-start.8
  141.4 72.4 %all-gather.9.cloned.1.call-start = ((), (), s32[]{:S(2)}) async-start(), calls=%async_computation.8 | async-start | bytes 2359296 | tf_op jit(solution)/shard_map/all_gather | solution.py:123
  142.1 100.9 %all-gather.7.cloned.1.call-start = ((), (), s32[]{:S(2)}) async-start(), calls=%async_computation.6 | async-start | bytes 2359296 | tf_op jit(solution)/shard_map/all_gather | solution.py:113
  189.0 95.4 %reduce-scatter.9.cloned.1.call-start = ((), (), s32[]{:S(2)}) async-start(), calls=%async_computation.9 | async-start | bytes 2359296 | tf_op jit(solution)/shard_map/reduce_scatter | solution.py:130
  258.2 54.5 %reduce-scatter.7.cloned.1.call-start = ((), (), s32[]{:S(2)}) async-start(), calls=%async_computation.7 | async-start | bytes 2359296 | tf_op jit(solution)/shard_map/reduce_scatter | solution.py:117
  266.7 17.8 %copy-start.10 = (f32[512,768]{1,0:T(8,128)S(1)}, f32[512,768]{1,0:T(8,128)}, u32[]{:S(2)}) copy-start(f32[512,768]{1,0:T(8,128)} %copy-done.9) | copy-start | bytes 4718596
  266.7 78.6 %all-gather.11.cloned.1.call-start = ((), (), s32[]{:S(2)}) async-start(), calls=%async_computation.10 | async-start | bytes 2359296 | tf_op jit(solution)/shard_map/all_gather | solution.py:140
  286.9 29.8 %copy-start.17 = (bf16[512,768]{1,0:T(8,128)(2,1)S(1)}, bf16[512,768]{1,0:T(8,128)(2,1)}, u32[]{:S(2)}) copy-start(bf16[512,768]{1,0:T(8,128)(2,1)} %param.17) | copy-start | bytes 2359300
  315.6 29.7 %copy-start.29 = (bf16[384,768]{1,0:T(8,128)(2,1)S(1)}, bf16[384,768]{1,0:T(8,128)(2,1)}, u32[]{:S(2)}) copy-start(bf16[384,768]{1,0:T(8,128)(2,1)} %param.24) | copy-start | bytes 1769476
  315.6 32.8 %copy-start.41 = (f32[512]{0:T(512)}, f32[512]{0:T(512)S(1)}, u32[]{:S(2)}) copy-start(f32[512]{0:T(512)S(1)} %negate_multiply_fusion.1) | copy-start | bytes 6148
  317.9 313.8 %reduce-scatter.11.cloned.1.call-start = ((), (), s32[]{:S(2)}) async-start(), calls=%async_computation.11 | async-start | bytes 2359296 | tf_op jit(solution)/shard_map/reduce_scatter | solution.py:191
  400.7 11.8 %copy-start.4 = (f32[6,512,1024]{2,1,0:T(8,128)S(1)}, f32[6,512,1024]{2,1,0:T(8,128)}, u32[]{:S(2)}) copy-start(f32[6,512,1024]{2,1,0:T(8,128)} %get-tuple-element.384) | copy-start | bytes 37748740 | tf_op jit(solution)/shard_map/while
  400.7 11.9 %copy-start.14 = (bf16[1024,6,64]{0,2,1:T(8,128)(2,1)S(1)}, bf16[1024,6,64]{0,2,1:T(8,128)(2,1)}, u32[]{:S(2)}) copy-start(bf16[1024,6,64]{0,2,1:T(8,128)(2,1)} %get-tuple-element.465) | copy-start | bytes 2359300 | tf_op jit(solution)/shard_map/while
  506.6 11.8 %copy-start.4 = (f32[6,512,1024]{2,1,0:T(8,128)S(1)}, f32[6,512,1024]{2,1,0:T(8,128)}, u32[]{:S(2)}) copy-start(f32[6,512,1024]{2,1,0:T(8,128)} %get-tuple-element.384) | copy-start | bytes 37748740 | tf_op jit(solution)/shard_map/while
  506.6 11.9 %copy-start.14 = (bf16[1024,6,64]{0,2,1:T(8,128)(2,1)S(1)}, bf16[1024,6,64]{0,2,1:T(8,128)(2,1)}, u32[]{:S(2)}) copy-start(bf16[1024,6,64]{0,2,1:T(8,128)(2,1)} %get-tuple-element.465) | copy-start | bytes 2359300 | tf_op jit(solution)/shard_map/while
  518.5 7.9 copy-start.2
  572.3 294.0 %all-reduce.4.cloned.1.call-start = ((), (), s32[]{:S(2)}) async-start(), calls=%async_computation.12 | async-start | bytes 28311552 | tf_op jit(solution)/shard_map/psum | solution.py:200
  579.7 8.8 copy-start.24
  579.7 8.8 copy-start.50
  596.4 35.3 %copy-start.12 = (bf16[512,768]{1,0:T(8,128)(2,1)S(1)}, bf16[512,768]{1,0:T(8,128)(2,1)}, u32[]{:S(2)}) copy-start(bf16[512,768]{1,0:T(8,128)(2,1)} %param.16) | copy-start | bytes 2359300
  596.4 35.3 %copy-start.36 = (f32[768]{0:T(1024)S(1)}, f32[768]{0:T(1024)}, u32[]{:S(2)}) copy-start(f32[768]{0:T(1024)} %copy-done.35) | copy-start | bytes 9220
  596.4 35.3 %copy-start.38 = (f32[512]{0:T(512)S(1)}, f32[512]{0:T(512)}, u32[]{:S(2)}) copy-start(f32[512]{0:T(512)} %copy-done.37) | copy-start | bytes 6148
  596.4 36.9 %copy-start.44 = (f32[512]{0:T(512)S(1)}, f32[512]{0:T(512)}, u32[]{:S(2)}) copy-start(f32[512]{0:T(512)} %copy-done.43) | copy-start | bytes 6148
  596.4 36.9 %copy-start.40 = (f32[512]{0:T(512)S(1)}, f32[512]{0:T(512)}, u32[]{:S(2)}) copy-start(f32[512]{0:T(512)} %copy-done.39) | copy-start | bytes 6148
  596.5 39.0 %copy-start.45 = (f32[768]{0:T(1024)S(1)}, f32[768]{0:T(1024)}, u32[]{:S(2)}) copy-start(f32[768]{0:T(1024)} %get-tuple-element.177) | copy-start | bytes 9220
  596.5 77.2 %copy-start.16 = (f32[512,768]{1,0:T(8,128)S(1)}, f32[512,768]{1,0:T(8,128)}, u32[]{:S(2)}) copy-start(f32[512,768]{1,0:T(8,128)} %copy-done.15) | copy-start | bytes 4718596
  596.5 77.2 %copy-start.18 = (bf16[512,768]{1,0:T(8,128)(2,1)S(1)}, bf16[512,768]{1,0:T(8,128)(2,1)}, u32[]{:S(2)}) copy-start(bf16[512,768]{1,0:T(8,128)(2,1)} %param.17) | copy-start | bytes 2359300
  596.5 77.2 %copy-start.42 = (f32[512]{0:T(512)S(1)}, f32[512]{0:T(512)}, u32[]{:S(2)}) copy-start(f32[512]{0:T(512)} %copy-done.41) | copy-start | bytes 6148
  (41 other events, 123.6 us)
Sparse Core Ops, SparseCore 0:
  13.4 29.8 all-gather.4
  141.5 43.3 reduce-scatter.4
  186.5 27.2 all-gather.8
  215.8 27.1 all-gather.6
  258.3 26.0 reduce-scatter.8
  286.5 26.0 reduce-scatter.6
  318.0 27.1 all-gather.10
  572.4 26.0 reduce-scatter.10
  604.8 261.4 all-reduce.3
where the time goes:
time: 891 us; the launch traced here: 885 us
  waiting for transfers between devices  380 us (43%)
  matrix products  245 us (27%)
  local copies, waits for them, and re-layouts  101 us (11%)
  blocking collectives  73.4 us (8%)
  other arithmetic  61 us (7%)
  between operations  14.6 us (2%)
  loops' own time  9.43 us (1%)
    psum x1, waiting for transfers between devices, body(): lax.psum((query_part, key_part, value_part, out_proj_grad, up_final, down...  190 us
    dot_general x4, matrix products, block_scores(): jnp.einsum('qhd,khd->hqk', query_block, key_heads, preferred_element_type...  58.2 us
    reduce_scatter x1, waiting for transfers between devices, body(): lax.psum_scatter(plain_times(attended, w_out), 'tensor', scatter_dimensio...  42.7 us
    psum x1, blocking collectives, body(): gain_sums = lax.psum((gain_one_part, gain_two_part), ('dp', 'tensor'))  38.2 us
    psum x1, blocking collectives, body(): lax.psum((query_part, key_part, value_part, out_proj_grad, up_final, down...  35.2 us
    dot_general x2, matrix products, attend_back(): jnp.einsum('hqk,qkm->hm', grad_scores, one_hot.astype(jnp.float32), preci...  34.8 us
    dot_general x4, matrix products, block_scores(): jnp.einsum('qkm,hm->hqk', one_hot, rel_table, preferred_element_type=jnp....  33.8 us
    mul x2, local copies, waits for them, and re-layouts, attend_back(): grad_scores = prob * (grad_prob - row_inner)  31.9 us
  transfers between devices with their start and end apart: 9, of which 8 were waited for; matrix products, arithmetic and copies ran while one was open for 6% of the time, Pallas kernels for 0%

commit v1 on v0

--- a/solution.py
+++ b/solution.py
@@ -201,7 +201,8 @@
         (query_part, key_part, value_part, out_proj_grad, up_final, down_final, table_part), "dp"
     )
     query_total, key_total, value_total, out_total, up_total, down_total, table_total = summed
-    gain_sums = lax.psum((gain_one_part, gain_two_part), ("dp", "tensor"))
+    partial = lax.psum((gain_one_part, gain_two_part), "tensor")
+    gain_sums = lax.psum(partial, "dp")
     return (
         out,
         input_grad,

time: 891 us -> 889 us (level)
  transfers between devices with their start and end apart: 9 -> 9, of which waited for: 8 -> 9; matrix products, arithmetic and copies ran while one was open for 6% -> 6% of each run, Pallas kernels for 0% -> 0%
where the time goes in v1:
time: 889 us; the launch traced here: 884 us
  waiting for transfers between devices  385 us (43%)
  matrix products  245 us (28%)
  local copies, waits for them, and re-layouts  101 us (11%)
  blocking collectives  68.5 us (8%)
  other arithmetic  60.8 us (7%)
  between operations  14.6 us (2%)
  loops' own time  9.03 us (1%)
    psum x1, waiting for transfers between devices, body(): lax.psum((query_part, key_part, value_part, out_proj_grad, up_final, down...  192 us
    psum x1, blocking collectives, body(): gain_sums = lax.psum(partial, 'dp')  63.5 us
    dot_general x4, matrix products, block_scores(): jnp.einsum('qhd,khd->hqk', query_block, key_heads, preferred_element_type...  58.3 us
    reduce_scatter x1, waiting for transfers between devices, body(): lax.psum_scatter(plain_times(attended, w_out), 'tensor', scatter_dimensio...  42.7 us
    dot_general x2, matrix products, attend_back(): jnp.einsum('hqk,qkm->hm', grad_scores, one_hot.astype(jnp.float32), preci...  34.8 us
    dot_general x4, matrix products, block_scores(): jnp.einsum('qkm,hm->hqk', one_hot, rel_table, preferred_element_type=jnp....  33.9 us
    mul x2, local copies, waits for them, and re-layouts, attend_back(): grad_scores = prob * (grad_prob - row_inner)  31.9 us
    dot_general x2, local copies, waits for them, and re-layouts, block_scores(): jnp.einsum('qkm,hm->hqk', one_hot, rel_table, preferred_element_type=jnp....  31.3 us
  transfers between devices with their start and end apart: 9, of which 9 were waited for; matrix products, arithmetic and copies ran while one was open for 6% of the time, Pallas kernels for 0%

profile of v1, /device:TPU:0, one launch (start us, length us, event | category | flops | bytes accessed | tf_op | source)
XLA Modules:
  0.0 884.2 jit_solution(16923370783971103217)
XLA Ops:
  13.7 29.7 %all-gather.5.cloned.1.call-done = bf16[1024,768]{1,0:T(8,128)(2,1)} async-done(((bf16[512,768]{1,0:T(8,128)(2,1)}), bf16[1024,768]{1,0:T(8,128)(2,1)}) %all-gather.5.cloned.1.call-update) | async-done | bytes 1572880 | tf_op jit(solution)/shard_map/all_gather | solution.py:71
  51.4 84.3 %while.29 = (s32[]{:T(128)}, bf16[2,512,6,64]{1,3,2,0:T(8,128)(2,1)}, f32[2,6,512]{2,1,0:T(8,128)S(1)}, s32[2]{0:T(128)S(1)}, s32[1024]{0:T(1024)S(1)}, /*index=...) while((s32[]{:T(128)}, ...), condition=%wide.region_7.8_spmd, body=%wide.region_4.7_spmd.sunk | while | flops 953901568 | bytes 133609992 | solution.py:106
  57.3 8.5 fusion.175
  65.7 15.3 %fusion.176 = (f32[6,512]{1,0:T(8,128)S(1)}, f32[6,512,1024]{2,1,0:T(8,128)S(1)}) fusion(f32[512,1024,6]{1,2,0:T(8,128)} %fusion.175, bf16[1024,6,64]{0,2,1:T(8,128)(2,1)S(1)} %get-tuple-element.419, bf16[1024,6,64]{0,2,1:T(8,128)(2,1)S(1)} %copy-done.8, s32[]{:T(128)S(6)} %select_n.59, pred[512,1024]{1,0:T(8,128)(4,1)S(1)} %broadcast_compare_fusion.4), kind=kOutput, calls=%fused_computation.146.clone.1 | convolution fusion | flops 415233024 | bytes 26882052 | tf_op jit(solution)/shard_map/while/body/eval_jaxpr/qhd,khd->hqk/dot_general | solution.py:84
  99.1 8.5 fusion.175
  107.6 15.3 %fusion.176 = (f32[6,512]{1,0:T(8,128)S(1)}, f32[6,512,1024]{2,1,0:T(8,128)S(1)}) fusion(f32[512,1024,6]{1,2,0:T(8,128)} %fusion.175, bf16[1024,6,64]{0,2,1:T(8,128)(2,1)S(1)} %get-tuple-element.419, bf16[1024,6,64]{0,2,1:T(8,128)(2,1)S(1)} %copy-done.8, s32[]{:T(128)S(6)} %select_n.59, pred[512,1024]{1,0:T(8,128)(4,1)S(1)} %broadcast_compare_fusion.4), kind=kOutput, calls=%fused_computation.146.clone.1 | convolution fusion | flops 415233024 | bytes 26882052 | tf_op jit(solution)/shard_map/while/body/eval_jaxpr/qhd,khd->hqk/dot_general | solution.py:84
  142.3 42.7 %reduce-scatter.5.cloned.1.call-done = f32[512,768]{1,0:T(8,128)} async-done(((f32[1024,768]{1,0:T(8,128)}), f32[512,768]{1,0:T(8,128)}) %reduce-scatter.5.cloned.1.call-update) | async-done | bytes 1572880 | tf_op jit(solution)/shard_map/reduce_scatter | solution.py:108
  189.2 24.7 %all-gather.9.cloned.1.call-done = bf16[1024,768]{1,0:T(8,128)(2,1)} async-done(((bf16[512,768]{1,0:T(8,128)(2,1)}), bf16[1024,768]{1,0:T(8,128)(2,1)}) %all-gather.9.cloned.1.call-update) | async-done | bytes 1572880 | tf_op jit(solution)/shard_map/all_gather | solution.py:123
  213.8 7.5 fusion.101
  221.3 21.8 %all-gather.7.cloned.1.call-done = bf16[1024,768]{1,0:T(8,128)(2,1)} async-done(((bf16[512,768]{1,0:T(8,128)(2,1)}), bf16[1024,768]{1,0:T(8,128)(2,1)}) %all-gather.7.cloned.1.call-update) | async-done | bytes 1572880 | tf_op jit(solution)/shard_map/all_gather | solution.py:113
  243.1 9.7 %fusion.77 = (bf16[1024,1536]{1,0:T(8,128)(2,1)S(1)}, f32[1024,1536]{1,0:T(8,128)}) fusion(f32[1024,1536]{1,0:T(8,128)} %fusion.101, bf16[1024,768]{1,0:T(8,128)(2,1)} %all-gather.7.cloned.1.call-done, bf16[768,1536]{1,0:T(8,128)(2,1)S(1)} %copy-done), kind=kOutput, calls=%fused_computation.91 | convolution fusion | flops 2447376384 | bytes 19660800 | tf_op jit(solution)/shard_map/dot_general | solution.py:22
  258.3 8.4 convolution_convert_fusion.1
  266.8 17.7 %reduce-scatter.9.cloned.1.call-done = bf16[512,768]{1,0:T(8,128)(2,1)} async-done(((bf16[1024,768]{1,0:T(8,128)(2,1)}), bf16[512,768]{1,0:T(8,128)(2,1)}) %reduce-scatter.9.cloned.1.call-update) | async-done | bytes 786448 | tf_op jit(solution)/shard_map/reduce_scatter | solution.py:130
  287.0 25.7 %reduce-scatter.7.cloned.1.call-done = bf16[512,768]{1,0:T(8,128)(2,1)} async-done(((bf16[1024,768]{1,0:T(8,128)(2,1)}), bf16[512,768]{1,0:T(8,128)(2,1)}) %reduce-scatter.7.cloned.1.call-update) | async-done | bytes 786448 | tf_op jit(solution)/shard_map/reduce_scatter | solution.py:117
  318.0 27.3 %all-gather.11.cloned.1.call-done = bf16[1024,768]{1,0:T(8,128)(2,1)} async-done(((bf16[512,768]{1,0:T(8,128)(2,1)}), bf16[1024,768]{1,0:T(8,128)(2,1)}) %all-gather.11.cloned.1.call-update) | async-done | bytes 1572880 | tf_op jit(solution)/shard_map/all_gather | solution.py:140
  349.4 214.1 %while.30 = (s32[]{:T(128)}, f32[1024,6,64]{0,2,1:T(8,128)}, f32[1024,6,64]{0,2,1:T(8,128)}, f32[6,16]{1,0:T(8,128)S(1)}, bf16[2,512,6,64]{1,3,2,0:T(8,128)(2,1)...) while((s32[]{:T(128)}, f32[1024,6,64]{0,2,1:T(8,128)}, ...), condition=%wide.region_17.18_spmd.clone, body=%wide.region_15.17_spmd.clone.sunk | while | flops 2483812096 | bytes 329461056 | solution.py:179
  362.5 8.5 fusion.192
  371.0 15.7 %copy.43 = f32[512,1024,6]{1,0,2:T(8,128)} copy(f32[512,1024,6]{0,2,1:T(8,128)} %fusion.192) | data formatting | bytes 25165824 | tf_op jit(solution)/shard_map/while/body/eval_jaxpr/qkm,hm->hqk/dot_general | solution.py:88
  386.7 13.8 %multiply_reduce_fusion.3 = (f32[6,512]{1,0:T(8,128)S(1)}, f32[6,512,1024]{2,1,0:T(8,128)}) fusion(f32[6,512,1024]{2,1,0:T(8,128)} %fusion.191, f32[6,512]{1,0:T(8,128)S(1)} %dynamic-slice_bitcast_fusion.2, f32[512,1024,6]{1,0,2:T(8,128)} %copy.43, bf16[1024,6,64]{0,2,1:T(8,128)(2,1)S(1)} %get-tuple-element.465, ...), kind=kOutput, calls=%fused_computation.44.clone.1 | convolution fusion | flops 421524480 | bytes 39477252 | tf_op jit(solution)/shard_map/while/body/eval_jaxpr/qhd,khd->hqk/dot_general | solution.py:84
  400.5 9.1 %subtract_multiply_fusion.2 = f32[6,512,1024]{2,1,0:T(8,128)S(1)} fusion(f32[6,512,1024]{2,1,0:T(8,128)} %get-tuple-element.387, f32[6,512,1024]{2,1,0:T(8,128)} %fusion.191, f32[6,512]{1,0:T(8,128)S(1)} %get-tuple-element.388), kind=kLoop, calls=%fused_computation.43.clone.1 | loop fusion | flops 6291456 | bytes 37761024 | tf_op jit(solution)/shard_map/while/body/eval_jaxpr/mul | solution.py:155
  421.8 16.0 %copy.44 = f32[6,512,1024]{1,0,2:T(8,128)} copy(f32[6,512,1024]{2,1,0:T(8,128)} %copy-done.2) | data formatting | bytes 25165824 | tf_op jit(solution)/shard_map/while/body/eval_jaxpr/mul | solution.py:155
  437.7 17.4 %fusion.193 = f32[6,16]{1,0:T(8,128)S(1)} fusion(f32[6,512,1024]{1,0,2:T(8,128)} %copy.44, s32[512,1024]{0,1:T(8,128)S(1)} %select_add_fusion.5, f32[6,16]{1,0:T(8,128)S(1)} %get-tuple-element.444, pred[]{:T(512)S(6)} %compare.3), kind=kOutput, calls=%fused_computation.69.clone.1 | convolution fusion | flops 310378688 | bytes 14680833 | tf_op jit(solution)/shard_map/while/body/eval_jaxpr/hqk,qkm->hm/dot_general | solution.py:156
  468.1 8.5 fusion.192
  476.6 15.7 %copy.43 = f32[512,1024,6]{1,0,2:T(8,128)} copy(f32[512,1024,6]{0,2,1:T(8,128)} %fusion.192) | data formatting | bytes 25165824 | tf_op jit(solution)/shard_map/while/body/eval_jaxpr/qkm,hm->hqk/dot_general | solution.py:88
  492.3 13.8 %multiply_reduce_fusion.3 = (f32[6,512]{1,0:T(8,128)S(1)}, f32[6,512,1024]{2,1,0:T(8,128)}) fusion(f32[6,512,1024]{2,1,0:T(8,128)} %fusion.191, f32[6,512]{1,0:T(8,128)S(1)} %dynamic-slice_bitcast_fusion.2, f32[512,1024,6]{1,0,2:T(8,128)} %copy.43, bf16[1024,6,64]{0,2,1:T(8,128)(2,1)S(1)} %get-tuple-element.465, ...), kind=kOutput, calls=%fused_computation.44.clone.1 | convolution fusion | flops 421524480 | bytes 39477252 | tf_op jit(solution)/shard_map/while/body/eval_jaxpr/qhd,khd->hqk/dot_general | solution.py:84
  506.1 9.1 %subtract_multiply_fusion.2 = f32[6,512,1024]{2,1,0:T(8,128)S(1)} fusion(f32[6,512,1024]{2,1,0:T(8,128)} %get-tuple-element.387, f32[6,512,1024]{2,1,0:T(8,128)} %fusion.191, f32[6,512]{1,0:T(8,128)S(1)} %get-tuple-element.388), kind=kLoop, calls=%fused_computation.43.clone.1 | loop fusion | flops 6291456 | bytes 37761024 | tf_op jit(solution)/shard_map/while/body/eval_jaxpr/mul | solution.py:155
  529.9 16.0 %copy.44 = f32[6,512,1024]{1,0,2:T(8,128)} copy(f32[6,512,1024]{2,1,0:T(8,128)} %copy-done.2) | data formatting | bytes 25165824 | tf_op jit(solution)/shard_map/while/body/eval_jaxpr/mul | solution.py:155
  545.9 17.4 %fusion.193 = f32[6,16]{1,0:T(8,128)S(1)} fusion(f32[6,512,1024]{1,0,2:T(8,128)} %copy.44, s32[512,1024]{0,1:T(8,128)S(1)} %select_add_fusion.5, f32[6,16]{1,0:T(8,128)S(1)} %get-tuple-element.444, pred[]{:T(512)S(6)} %compare.3), kind=kOutput, calls=%fused_computation.69.clone.1 | convolution fusion | flops 310378688 | bytes 14680833 | tf_op jit(solution)/shard_map/while/body/eval_jaxpr/hqk,qkm->hm/dot_general | solution.py:156
  571.9 7.3 fusion.108
  579.2 8.8 fusion.96
  606.8 63.5 %all-reduce = (f32[768]{0:T(1024)}, f32[768]{0:T(1024)}, f32[6,16]{1,0:T(8,128)}) all-reduce(f32[768]{0:T(1024)S(1)} %get-tuple-element.234, f32[768]{0:T(1024)S(1)} %get-tuple-element.235, f32[6,16]{1,0:T(8,128)S(1)} %get-tuple-element.134), channel_id=1, replica_groups=mesh['dp'=16,'tensor'=2] {'dp'}, use_global_device_ids=true, to_apply=%region_23.24 | all-reduce | flops 1632 | bytes 13056 | tf_op jit(solution)/shard_map/psum | solution.py:205
  673.1 192.2 %all-reduce.5.cloned.1.call-done = (f32[768,384]{1,0:T(8,128)}, f32[768,384]{1,0:T(8,128)}, f32[768,384]{1,0:T(8,128)}, f32[384,768]{1,0:T(8,128)}, f32[768,1536]{1,0:T(8,128)}, /*index=5*/f32[1536,768]{1,0:T(8,128)}) async-done(((f32[768,384]{1,0:T(8,128)}, f32[768,384]{1,0:T(8,128)}, f32[768,384]{1,0:T(8,128)}, f32[384,768]{1,0:T(8,128)}, f32[768,1536]{1,0:T(8,128)}, /*index=5*/f32[1536,768]{1,0:T(8,128)}), ...) | async-done | bytes 14155792 | tf_op jit(solution)/shard_map/psum | solution.py:200
  (245 shorter events, 165.0 us)
Async XLA Ops:
  7.2 236.0 %copy-start = (bf16[768,1536]{1,0:T(8,128)(2,1)S(1)}, bf16[768,1536]{1,0:T(8,128)(2,1)}, u32[]{:S(2)}) copy-start(bf16[768,1536]{1,0:T(8,128)(2,1)} %param.25) | copy-start | bytes 7077892
  7.2 4.9 copy-start.11
  7.2 6.2 copy-start.51
  7.2 36.2 %all-gather.5.cloned.1.call-start = ((), (), s32[]{:S(2)}) async-start(), calls=%async_computation.4 | async-start | bytes 2359296 | tf_op jit(solution)/shard_map/all_gather | solution.py:71
  13.3 171.7 %reduce-scatter.5.cloned.1.call-start = ((), (), s32[]{:S(2)}) async-start(), calls=%async_computation.5 | async-start | bytes 4718592 | tf_op jit(solution)/shard_map/reduce_scatter | solution.py:108
  57.3 8.5 copy-start.8
  99.1 8.5 copy-start.8
  122.9 4.7 copy-start.3
  141.5 72.4 %all-gather.9.cloned.1.call-start = ((), (), s32[]{:S(2)}) async-start(), calls=%async_computation.8 | async-start | bytes 2359296 | tf_op jit(solution)/shard_map/all_gather | solution.py:123
  142.2 100.9 %all-gather.7.cloned.1.call-start = ((), (), s32[]{:S(2)}) async-start(), calls=%async_computation.6 | async-start | bytes 2359296 | tf_op jit(solution)/shard_map/all_gather | solution.py:113
  189.1 95.4 %reduce-scatter.9.cloned.1.call-start = ((), (), s32[]{:S(2)}) async-start(), calls=%async_computation.9 | async-start | bytes 2359296 | tf_op jit(solution)/shard_map/reduce_scatter | solution.py:130
  258.3 54.4 %reduce-scatter.7.cloned.1.call-start = ((), (), s32[]{:S(2)}) async-start(), calls=%async_computation.7 | async-start | bytes 2359296 | tf_op jit(solution)/shard_map/reduce_scatter | solution.py:117
  266.8 17.8 %copy-start.10 = (f32[512,768]{1,0:T(8,128)S(1)}, f32[512,768]{1,0:T(8,128)}, u32[]{:S(2)}) copy-start(f32[512,768]{1,0:T(8,128)} %copy-done.9) | copy-start | bytes 4718596
  266.8 78.6 %all-gather.11.cloned.1.call-start = ((), (), s32[]{:S(2)}) async-start(), calls=%async_computation.10 | async-start | bytes 2359296 | tf_op jit(solution)/shard_map/all_gather | solution.py:140
  287.0 29.8 %copy-start.17 = (bf16[512,768]{1,0:T(8,128)(2,1)S(1)}, bf16[512,768]{1,0:T(8,128)(2,1)}, u32[]{:S(2)}) copy-start(bf16[512,768]{1,0:T(8,128)(2,1)} %param.17) | copy-start | bytes 2359300
  315.7 29.7 %copy-start.29 = (bf16[384,768]{1,0:T(8,128)(2,1)S(1)}, bf16[384,768]{1,0:T(8,128)(2,1)}, u32[]{:S(2)}) copy-start(bf16[384,768]{1,0:T(8,128)(2,1)} %param.24) | copy-start | bytes 1769476
  315.7 32.8 %copy-start.41 = (f32[512]{0:T(512)}, f32[512]{0:T(512)S(1)}, u32[]{:S(2)}) copy-start(f32[512]{0:T(512)S(1)} %negate_multiply_fusion.1) | copy-start | bytes 6148
  318.0 280.1 %reduce-scatter.11.cloned.1.call-start = ((), (), s32[]{:S(2)}) async-start(), calls=%async_computation.11 | async-start | bytes 2359296 | tf_op jit(solution)/shard_map/reduce_scatter | solution.py:191
  400.5 11.8 %copy-start.4 = (f32[6,512,1024]{2,1,0:T(8,128)S(1)}, f32[6,512,1024]{2,1,0:T(8,128)}, u32[]{:S(2)}) copy-start(f32[6,512,1024]{2,1,0:T(8,128)} %get-tuple-element.387) | copy-start | bytes 37748740 | tf_op jit(solution)/shard_map/while
  400.5 11.9 %copy-start.14 = (bf16[1024,6,64]{0,2,1:T(8,128)(2,1)S(1)}, bf16[1024,6,64]{0,2,1:T(8,128)(2,1)}, u32[]{:S(2)}) copy-start(bf16[1024,6,64]{0,2,1:T(8,128)(2,1)} %get-tuple-element.468) | copy-start | bytes 2359300 | tf_op jit(solution)/shard_map/while
  412.5 5.8 copy-start.2
  506.1 11.8 %copy-start.4 = (f32[6,512,1024]{2,1,0:T(8,128)S(1)}, f32[6,512,1024]{2,1,0:T(8,128)}, u32[]{:S(2)}) copy-start(f32[6,512,1024]{2,1,0:T(8,128)} %get-tuple-element.387) | copy-start | bytes 37748740 | tf_op jit(solution)/shard_map/while
  506.1 11.9 %copy-start.14 = (bf16[1024,6,64]{0,2,1:T(8,128)(2,1)S(1)}, bf16[1024,6,64]{0,2,1:T(8,128)(2,1)}, u32[]{:S(2)}) copy-start(bf16[1024,6,64]{0,2,1:T(8,128)(2,1)} %get-tuple-element.468) | copy-start | bytes 2359300 | tf_op jit(solution)/shard_map/while
  518.0 7.9 copy-start.2
  571.9 293.4 %all-reduce.5.cloned.1.call-start = ((), (), s32[]{:S(2)}) async-start(), calls=%async_computation.12 | async-start | bytes 28311552 | tf_op jit(solution)/shard_map/psum | solution.py:200
  571.9 7.3 copy-start.49
  579.2 8.8 copy-start.24
  579.2 8.8 copy-start.50
  596.0 5.8 copy-start.45
  596.0 74.3 %copy-start.16 = (f32[512,768]{1,0:T(8,128)S(1)}, f32[512,768]{1,0:T(8,128)}, u32[]{:S(2)}) copy-start(f32[512,768]{1,0:T(8,128)} %copy-done.15) | copy-start | bytes 4718596
  596.0 74.3 %copy-start.18 = (bf16[512,768]{1,0:T(8,128)(2,1)S(1)}, bf16[512,768]{1,0:T(8,128)(2,1)}, u32[]{:S(2)}) copy-start(bf16[512,768]{1,0:T(8,128)(2,1)} %param.17) | copy-start | bytes 2359300
  596.0 74.3 %copy-start.42 = (f32[512]{0:T(512)S(1)}, f32[512]{0:T(512)}, u32[]{:S(2)}) copy-start(f32[512]{0:T(512)} %copy-done.41) | copy-start | bytes 6148
  (41 other events, 108.3 us)
Sparse Core Ops, SparseCore 0:
  13.4 29.8 all-gather.4
  141.6 43.3 reduce-scatter.4
  186.6 27.2 all-gather.8
  215.9 27.1 all-gather.6
  258.4 26.0 reduce-scatter.8
  286.6 26.0 reduce-scatter.6
  318.1 27.2 all-gather.10
  572.0 26.0 reduce-scatter.10
  604.4 260.8 all-reduce.4
